TPU v7x, 128 devices: a whole 4x4x4 slice. The times are simulated.
128 devices in a mesh: row: 16 (over x, z), col: 4 (over y_hi, core), tm: 2 (over y_lo).
Axes of the slice: x: 4, y: 4 (y_hi: 2, y_lo: 2; y = y_hi * 2 + y_lo), z: 4, core: 2. Of those that a mesh axis runs over, the one named last changes fastest.
Arguments:
- samples: bfloat16 [1024, 16, 2, 4096], P('row', None, 'tm', 'col'), may hold values from -6 to 6
- whitening: bfloat16 [1024, 1024], replicated, may hold values from -0.1875 to 0.1875
- ridge: float32 [2048], P('col'), may hold values from 2 to 20
- slab_start: int32 [1], replicated, may hold values from 0 to 63
- panels: int32 [4], replicated, may hold values from 0 to 3, as said below
Outputs:
- trailing: float32 [131072, 2048], P(('row', 'tm'), 'col')
- factor: bfloat16 [2, 131072, 512], P(None, ('row', 'tm'))
Inputs may be any that keep to these rules, and one draw needn't show every extreme that they name: `panels`: each panel index once.
All inputs are finite; a program needn't handle non-finite values.
Results may differ from a plain program's by a relative error of at most 0.012.
The roundings to bfloat16 on the way count: a program that leaves them out, or rounds other values in their place, can miss the bound.
Values may be sent and summed in bfloat16 or wider, within the bound.
No kernel may reach another device: no remote copies, remote signals or barrier semaphores. Data moves between devices by JAX's collectives and lax.ppermute only.
A program may use at most 192 MiB of HBM per device.

v0:
```python
import jax
import jax.numpy as jnp
from jax import lax
from jax.sharding import PartitionSpec as P

S = 1024
PANEL = 512
PANELS = 2


def broadcast(block, axis, holder):
    block = jnp.where(lax.axis_index(axis) == holder, block, jnp.zeros_like(block))
    return lax.psum(block, axis)


def rows_for(lines, devices):
    spare = -lines.shape[0] % devices
    if not spare:
        return lines
    return jnp.concatenate([lines, jnp.zeros((spare, *lines.shape[1:]), lines.dtype)])


def from_root(shard, axis, root):
    lines = jnp.where(lax.axis_index(axis) == root, shard, jnp.zeros_like(shard)).reshape(
        -1, *shard.shape[1:][-1:]
    )
    padded = rows_for(lines, lax.axis_size(axis))
    own = lax.psum_scatter(padded, axis, scatter_dimension=0, tiled=True)
    return lax.all_gather(own, axis, axis=0, tiled=True)[: len(lines)].reshape(shard.shape)


def broadcast_2(shard, axis, root):
    return lax.dynamic_index_in_dim(lax.all_gather(shard, axis), root, 0, keepdims=False)


def on_device(samples, whitening, ridge, slab_start, panels):
    moved = lax.all_to_all(samples, "row", split_axis=1, concat_axis=0, tiled=True)
    local_width = moved.shape[3]
    series = moved.reshape(moved.shape[0], local_width)
    whitened = jnp.dot(whitening, series, preferred_element_type=jnp.float32).astype(jnp.bfloat16)
    col_count = lax.axis_size("col")
    tm_count = lax.axis_size("tm")
    rows_here = col_count * local_width
    slab_width = PANEL * col_count
    scale = S ** (-0.5)
    slab_first = slab_start[0] * slab_width
    owner_index = slab_first // rows_here
    slab_offset = slab_first % rows_here
    col_index = lax.axis_index("col")
    self_index = lax.axis_index("row") * tm_count + lax.axis_index("tm")
    row_series = lax.all_gather(whitened, "col", axis=1, tiled=True)
    piece = lax.dynamic_slice_in_dim(row_series, slab_offset + col_index * PANEL, PANEL, 1)
    slab_part = broadcast(piece, ("row", "tm"), owner_index)
    covariance = (
        lax.dot_general(
            row_series, slab_part, (((0,), (0,)), ((), ())), preferred_element_type=jnp.float32
        )
        * scale
    )
    owner_flag = (self_index == owner_index).astype(jnp.float32)
    ridge_rows = slab_offset + col_index * PANEL
    zero_index = jnp.zeros((), jnp.int32)
    diag_block = (
        lax.dynamic_slice(covariance, (ridge_rows, zero_index), (PANEL, PANEL))
        + jnp.diag(ridge) * owner_flag
    )
    covariance = lax.dynamic_update_slice(covariance, diag_block, (ridge_rows, zero_index))
    identity = jnp.eye(PANEL, dtype=jnp.float32)
    factors = []
    finished = col_index < 0
    for section in range(PANELS):
        panel_index = panels[section]
        finished = finished | (col_index == panel_index)
        pivot_local = lax.dynamic_slice_in_dim(
            covariance, slab_offset + panel_index * PANEL, PANEL, 0
        )
        pivot_rows = from_root(pivot_local, ("row", "tm"), owner_index)
        pivot_safe = jnp.where(col_index == panel_index, pivot_rows, identity)
        lower_factor = jnp.linalg.cholesky(pivot_safe)
        panel_now = jax.scipy.linalg.solve_triangular(lower_factor, covariance.T, lower=True).T
        small_block = lower_factor
        panel_bf = broadcast_2(panel_now.astype(jnp.bfloat16), "col", panel_index)
        small_block = broadcast_2(small_block, "col", panel_index)
        coupling = jax.scipy.linalg.solve_triangular(small_block, pivot_rows, lower=True).T
        coupling_bf = coupling.astype(jnp.bfloat16)
        covariance = covariance - lax.dot_general(
            panel_bf, coupling_bf, (((1,), (1,)), ((), ())), preferred_element_type=jnp.float32
        )
        factors.append(panel_bf)
    trailing = jnp.where(finished, jnp.zeros_like(covariance), covariance)
    return (trailing, jnp.stack(factors))


def solution(mesh):
    in_specs = (P("row", None, "tm", "col"), P(), P("col"), P(), P())
    out_specs = (P(("row", "tm"), "col"), P(None, ("row", "tm"), None))
    return jax.shard_map(
        on_device, mesh=mesh, in_specs=in_specs, out_specs=out_specs, check_vma=False
    )
```

profile of v0, /device:TPU:1, one launch (start us, length us, event | category | flops | bytes accessed | tf_op | source)
XLA Modules:
  0.0 1696.4 jit_solution(11098721160999571711)
XLA Ops:
  10.1 34.7 %all_to_all.15 = bf16[64,16,1,1024]{3,0,2,1:T(8,128)(2,1)S(1)} all-to-all(bf16[64,16,1,1024]{3,0,2,1:T(8,128)(2,1)S(1)} %copy.24), channel_id=1, replica_groups=mesh['row'=16,'col'=4,'tm'=2] {'row'}, dimensions={1} | all-to-all | bytes 4194304 | tf_op jit(solution)/shard_map/all_to_all | solution.py:37
  49.3 62.6 %all-gather.12.cloned.1.call-done = bf16[1024,4096]{1,0:T(8,128)(2,1)} async-done(((bf16[1024,1024]{1,0:T(8,128)(2,1)}), bf16[1024,4096]{1,0:T(8,128)(2,1)}) %all-gather.12.cloned.1.call-update) | async-done | bytes 8388624 | tf_op jit(solution)/shard_map/all_gather | solution.py:51
  116.0 284.7 %all-reduce.3.cloned.1.call-done = bf16[1024,512]{1,0:T(8,128)(2,1)} async-done(((bf16[1024,512]{1,0:T(8,128)(2,1)}), bf16[1024,512]{1,0:T(8,128)(2,1)}) %all-reduce.3.cloned.1.call-update) | async-done | bytes 1048592 | tf_op jit(solution)/shard_map/psum | solution.py:13
  420.8 160.0 %reduce-scatter.7.cloned.1.call-done = f32[16,512]{1,0:T(8,128)} async-done(((f32[512,512]{1,0:T(8,128)}), f32[16,512]{1,0:T(8,128)}) %reduce-scatter.7.cloned.1.call-update) | async-done | bytes 32784 | tf_op jit(solution)/shard_map/reduce_scatter | solution.py:28
  581.7 149.1 %all-gather.14.cloned.1.call-done = f32[512,512]{1,0:T(8,128)} async-done(((f32[16,512]{1,0:T(8,128)}), f32[512,512]{1,0:T(8,128)}) %all-gather.14.cloned.1.call-update) | async-done | bytes 1048592 | tf_op jit(solution)/shard_map/all_gather | solution.py:29
  733.1 11.7 cholesky.286
  744.8 9.8 custom-call.31
  755.5 11.7 cholesky.305
  767.2 10.2 custom-call.32
  778.1 11.7 cholesky.326
  790.5 9.8 custom-call.33
  800.9 11.9 cholesky.343
  826.0 39.3 %custom-call.34 = f32[4,128,128]{1,2,0:T(8,128)S(1)} custom-call(f32[4,128,128]{2,1,0:T(8,128)S(1)} %get-tuple-element.33), custom_call_target="InvertDiagBlocksLowerTriangular" | custom-call | tf_op jit(solution)/shard_map/jit(_solve_triangular)/triangular_solve | solution.py:80
  902.4 39.3 %custom-call.35 = f32[4,128,128]{1,2,0:T(8,128)S(1)} custom-call(f32[4,128,128]{2,1,0:T(8,128)S(1)} %get-tuple-element.34), custom_call_target="InvertDiagBlocksLowerTriangular" | custom-call | tf_op jit(solution)/shard_map/jit(_solve_triangular)/triangular_solve | solution.py:84
  944.8 78.1 %all-gather.18.cloned.1.call-done = bf16[16384,512]{0,1:T(8,128)(2,1)} async-done(((bf16[4096,512]{0,1:T(8,128)(2,1)}), bf16[16384,512]{0,1:T(8,128)(2,1)}) %all-gather.18.cloned.1.call-update) | async-done | bytes 16777232 | tf_op jit(solution)/shard_map/all_gather | solution.py:33
  1022.9 22.4 %copy.40 = bf16[16384,512]{1,0:T(8,128)(2,1)} copy(bf16[16384,512]{0,1:T(8,128)(2,1)} %all-gather.18.cloned.1.call-done) | data formatting | bytes 33554432 | tf_op jit(solution)/shard_map/all_gather | solution.py:33
  1060.6 136.3 %reduce-scatter.9.cloned.1.call-done = f32[16,512]{1,0:T(8,128)} async-done(((f32[512,512]{1,0:T(8,128)}), f32[16,512]{1,0:T(8,128)}) %reduce-scatter.9.cloned.1.call-update) | async-done | bytes 32784 | tf_op jit(solution)/shard_map/reduce_scatter | solution.py:28
  1197.7 149.6 %all-gather.16.cloned.1.call-done = f32[512,512]{1,0:T(8,128)} async-done(((f32[16,512]{1,0:T(8,128)}), f32[512,512]{1,0:T(8,128)}) %all-gather.16.cloned.1.call-update) | async-done | bytes 1048592 | tf_op jit(solution)/shard_map/all_gather | solution.py:29
  1349.6 11.7 cholesky.358
  1362.0 9.8 custom-call.36
  1372.6 11.7 cholesky.377
  1385.1 10.2 custom-call.37
  1395.9 11.7 cholesky.398
  1408.3 9.8 custom-call.38
  1418.8 11.9 cholesky.415
  1442.8 39.3 %custom-call.39 = f32[4,128,128]{1,2,0:T(8,128)S(1)} custom-call(f32[4,128,128]{2,1,0:T(8,128)S(1)} %get-tuple-element.35), custom_call_target="InvertDiagBlocksLowerTriangular" | custom-call | tf_op jit(solution)/shard_map/jit(_solve_triangular)/triangular_solve | solution.py:80
  1510.5 8.3 while.11
  1518.8 39.3 %custom-call.40 = f32[4,128,128]{1,2,0:T(8,128)S(1)} custom-call(f32[4,128,128]{2,1,0:T(8,128)S(1)} %get-tuple-element.36), custom_call_target="InvertDiagBlocksLowerTriangular" | custom-call | tf_op jit(solution)/shard_map/jit(_solve_triangular)/triangular_solve | solution.py:84
  1561.3 78.4 %all-gather.22.cloned.1.call-done = bf16[16384,512]{0,1:T(8,128)(2,1)} async-done(((bf16[4096,512]{0,1:T(8,128)(2,1)}), bf16[16384,512]{0,1:T(8,128)(2,1)}) %all-gather.22.cloned.1.call-update) | async-done | bytes 16777232 | tf_op jit(solution)/shard_map/all_gather | solution.py:33
  1639.7 22.6 %copy.41 = bf16[16384,512]{1,0:T(8,128)(2,1)} copy(bf16[16384,512]{0,1:T(8,128)(2,1)} %all-gather.22.cloned.1.call-done) | data formatting | bytes 33554432 | tf_op jit(solution)/shard_map/all_gather | solution.py:33
  1671.2 9.0 subtract_select_fusion
  1680.2 9.1 copy.36
  (189 shorter events, 185.2 us)
Async XLA Ops:
  7.2 37.7 %copy-start = (bf16[1024,1024]{1,0:T(8,128)(2,1)S(1)}, bf16[1024,1024]{1,0:T(8,128)(2,1)}, u32[]{:S(2)}) copy-start(bf16[1024,1024]{1,0:T(8,128)(2,1)} %param.11) | copy-start | bytes 6291460
  7.2 104.7 %all-gather.12.cloned.1.call-start = ((), (), s32[]{:S(2)}) async-start(), calls=%async_computation.3 | async-start | bytes 10485760 | tf_op jit(solution)/shard_map/all_gather | solution.py:51
  48.5 66.2 %copy-start.8 = (s32[4]{0:T(128)S(1)}, s32[4]{0:T(128)}, u32[]{:S(2)}) copy-start(s32[4]{0:T(128)} %param.14) | copy-start | bytes 52
  48.5 352.1 %all-reduce.3.cloned.1.call-start = ((), (), s32[]{:S(2)}) async-start(), calls=%async_computation.4 | async-start | bytes 2097152 | tf_op jit(solution)/shard_map/psum | solution.py:13
  114.7 466.1 %reduce-scatter.7.cloned.1.call-start = ((), (), s32[]{:S(2)}) async-start(), calls=%async_computation.11 | async-start | bytes 1081344 | tf_op jit(solution)/shard_map/reduce_scatter | solution.py:28
  116.0 295.6 %copy-start.7 = (f32[512]{0:T(512)S(1)}, f32[512]{0:T(512)}, u32[]{:S(2)}) copy-start(f32[512]{0:T(512)} %param.12) | copy-start | bytes 6148
  408.2 3.4 copy-start.3
  420.8 310.0 %all-gather.14.cloned.1.call-start = ((), (), s32[]{:S(2)}) async-start(), calls=%async_computation.5 | async-start | bytes 1081344 | tf_op jit(solution)/shard_map/all_gather | solution.py:29
  580.9 312.3 %all-gather.20.cloned.1.call-start = ((), (), s32[]{:S(2)}) async-start(), calls=%async_computation.8 | async-start | bytes 5242880 | tf_op jit(solution)/shard_map/all_gather | solution.py:33
  817.9 205.1 %all-gather.18.cloned.1.call-start = ((), (), s32[]{:S(2)}) async-start(), calls=%async_computation.7 | async-start | bytes 20971520 | tf_op jit(solution)/shard_map/all_gather | solution.py:33
  890.6 51.0 %copy-start.5 = (f32[512,512]{1,0:T(8,128)S(1)}, f32[512,512]{1,0:T(8,128)}, u32[]{:S(2)}) copy-start(f32[512,512]{1,0:T(8,128)} %all-gather.14.cloned.1.call-done) | copy-start | bytes 3145732
  890.7 306.2 %reduce-scatter.9.cloned.1.call-start = ((), (), s32[]{:S(2)}) async-start(), calls=%async_computation.12 | async-start | bytes 1081344 | tf_op jit(solution)/shard_map/reduce_scatter | solution.py:28
  1047.8 7.6 copy-start.4
  1055.4 3.4 copy-start.2
  1060.5 286.8 %all-gather.16.cloned.1.call-start = ((), (), s32[]{:S(2)}) async-start(), calls=%async_computation.6 | async-start | bytes 1081344 | tf_op jit(solution)/shard_map/all_gather | solution.py:29
  1196.9 312.3 %all-gather.24.cloned.1.call-start = ((), (), s32[]{:S(2)}) async-start(), calls=%async_computation.10 | async-start | bytes 5242880 | tf_op jit(solution)/shard_map/all_gather | solution.py:33
  1435.0 204.7 %all-gather.22.cloned.1.call-start = ((), (), s32[]{:S(2)}) async-start(), calls=%async_computation.9 | async-start | bytes 20971520 | tf_op jit(solution)/shard_map/all_gather | solution.py:33
  1507.1 51.0 %copy-start.6 = (f32[512,512]{1,0:T(8,128)S(1)}, f32[512,512]{1,0:T(8,128)}, u32[]{:S(2)}) copy-start(f32[512,512]{1,0:T(8,128)} %all-gather.16.cloned.1.call-done) | copy-start | bytes 3145732
  1680.2 9.1 copy-start.1
Sparse Core Ops, SparseCore 0:
  48.7 63.1 all-gather.11
  114.9 285.7 all-reduce.2
  420.9 159.9 reduce-scatter.6
  582.3 148.4 all-gather.13
  818.0 60.6 all-gather.19
  890.8 132.0 all-gather.17
  1060.6 136.1 reduce-scatter.8
  1198.6 148.7 all-gather.15
  1435.2 61.2 all-gather.23
  1507.3 132.3 all-gather.21
where the time goes:
time: 1700 us
  waiting for transfers between devices  1100 us (65%)
  other arithmetic  338 us (20%)
  local copies, waits for them, and re-layouts  113 us (7%)
  matrix products  83.3 us (5%)
  blocking collectives  34.7 us (2%)
  between operations  26.9 us (2%)
    all_gather x2, waiting for transfers between devices, from_root(): lax.all_gather(own, axis, axis=0, tiled=True)[:len(lines)]  299 us
    reduce_scatter x2, waiting for transfers between devices, from_root(): own = lax.psum_scatter(padded, axis, scatter_dimension=0, tiled=True)  296 us
    psum x1, waiting for transfers between devices, broadcast(): return lax.psum(block, axis)  285 us
    another operation x29, other arithmetic, on_device(): lower_factor = jnp.linalg.cholesky(pivot_safe)  158 us
    all_gather x4, waiting for transfers between devices, broadcast_2(): lax.all_gather(shard, axis)  157 us
    another operation x4, other arithmetic, on_device(): jax.scipy.linalg.solve_triangular(small_block, pivot_rows, lower=True)  81.3 us
    another operation x5, other arithmetic, on_device(): jax.scipy.linalg.solve_triangular(lower_factor, covariance.T, lower=True)  81.2 us
    all_gather x1, waiting for transfers between devices, on_device(): row_series = lax.all_gather(whitened, 'col', axis=1, tiled=True)  62.6 us
  transfers between devices with their start and end apart: 10, of which 8 were waited for; matrix products, arithmetic and copies ran while one was open for 15% of the time, Pallas kernels for 0%

commit v1 on v0

--- a/solution.py
+++ b/solution.py
@@ -10,7 +10,7 @@
 
 def broadcast(block, axis, holder):
     block = jnp.where(lax.axis_index(axis) == holder, block, jnp.zeros_like(block))
-    return lax.psum(block, axis)
+    return jnp.sum(jax.lax.all_gather(block, axis_name=axis), axis=0)
 
 
 def rows_for(lines, devices):

time: 1700 us -> 2120 us (1.25)
  waiting for transfers between devices: 1100 us -> 1500 us
    all_gather x0 -> x1, waiting for transfers between devices: none -> 706 us  [broadcast(): return jnp.sum(jax.lax.all_gather(block, axis_name=axis), axis=0)]
    psum x1 -> x0, waiting for transfers between devices: 285 us -> none  [broadcast(): return lax.psum(block, axis)]
  transfers between devices with their start and end apart: 10 -> 10, of which waited for: 8 -> 8; matrix products, arithmetic and copies ran while one was open for 15% -> 12% of each run, Pallas kernels for 0% -> 0%
where the time goes in v1:
time: 2120 us; the launch traced here: 2110 us
  waiting for transfers between devices  1500 us (71%)
  other arithmetic  350 us (17%)
  local copies, waits for them, and re-layouts  114 us (5%)
  matrix products  83 us (4%)
  blocking collectives  34.7 us (2%)
  between operations  27.8 us (1%)
    all_gather x1, waiting for transfers between devices, broadcast(): return jnp.sum(jax.lax.all_gather(block, axis_name=axis), axis=0)  706 us
    all_gather x2, waiting for transfers between devices, from_root(): lax.all_gather(own, axis, axis=0, tiled=True)[:len(lines)]  302 us
    reduce_scatter x2, waiting for transfers between devices, from_root(): own = lax.psum_scatter(padded, axis, scatter_dimension=0, tiled=True)  275 us
    another operation x29, other arithmetic, on_device(): lower_factor = jnp.linalg.cholesky(pivot_safe)  159 us
    all_gather x4, waiting for transfers between devices, broadcast_2(): lax.all_gather(shard, axis)  156 us
    another operation x4, other arithmetic, on_device(): jax.scipy.linalg.solve_triangular(small_block, pivot_rows, lower=True)  81.3 us
    another operation x5, other arithmetic, on_device(): jax.scipy.linalg.solve_triangular(lower_factor, covariance.T, lower=True)  81.2 us
    all_gather x1, waiting for transfers between devices, on_device(): row_series = lax.all_gather(whitened, 'col', axis=1, tiled=True)  62.6 us
  transfers between devices with their start and end apart: 10, of which 8 were waited for; matrix products, arithmetic and copies ran while one was open for 12% of the time, Pallas kernels for 0%

profile of v1, /device:TPU:1, one launch (start us, length us, event | category | flops | bytes accessed | tf_op | source)
XLA Modules:
  0.0 2112.3 jit_solution(8425039882487554838)
XLA Ops:
  10.1 34.7 %all_to_all.15 = bf16[64,16,1,1024]{3,0,2,1:T(8,128)(2,1)S(1)} all-to-all(bf16[64,16,1,1024]{3,0,2,1:T(8,128)(2,1)S(1)} %copy.24), channel_id=1, replica_groups=mesh['row'=16,'col'=4,'tm'=2] {'row'}, dimensions={1} | all-to-all | bytes 4194304 | tf_op jit(solution)/shard_map/all_to_all | solution.py:37
  49.3 62.6 %all-gather.14.cloned.1.call-done = bf16[1024,4096]{1,0:T(8,128)(2,1)} async-done(((bf16[1024,1024]{1,0:T(8,128)(2,1)}), bf16[1024,4096]{1,0:T(8,128)(2,1)}) %all-gather.14.cloned.1.call-update) | async-done | bytes 8388624 | tf_op jit(solution)/shard_map/all_gather | solution.py:51
  116.1 706.4 %all-gather.20.cloned.1.call-done = bf16[32768,512]{1,0:T(8,128)(2,1)} async-done(((bf16[1024,512]{1,0:T(8,128)(2,1)}), bf16[32768,512]{1,0:T(8,128)(2,1)}) %all-gather.20.cloned.1.call-update) | async-done | bytes 33554448 | tf_op jit(solution)/shard_map/all_gather | solution.py:13
  822.5 11.4 reduce_sum.12
  853.8 140.0 %reduce-scatter.7.cloned.1.call-done = f32[16,512]{1,0:T(8,128)} async-done(((f32[512,512]{1,0:T(8,128)}), f32[16,512]{1,0:T(8,128)}) %reduce-scatter.7.cloned.1.call-update) | async-done | bytes 32784 | tf_op jit(solution)/shard_map/reduce_scatter | solution.py:28
  994.8 150.7 %all-gather.16.cloned.1.call-done = f32[512,512]{1,0:T(8,128)} async-done(((f32[16,512]{1,0:T(8,128)}), f32[512,512]{1,0:T(8,128)}) %all-gather.16.cloned.1.call-update) | async-done | bytes 1048592 | tf_op jit(solution)/shard_map/all_gather | solution.py:29
  1147.7 11.7 cholesky.286
  1159.5 9.8 custom-call.31
  1170.1 11.7 cholesky.305
  1181.8 10.2 custom-call.32
  1192.8 11.7 cholesky.326
  1205.2 9.8 custom-call.33
  1215.6 11.9 cholesky.343
  1240.2 39.3 %custom-call.34 = f32[4,128,128]{1,2,0:T(8,128)S(1)} custom-call(f32[4,128,128]{2,1,0:T(8,128)S(1)} %get-tuple-element.33), custom_call_target="InvertDiagBlocksLowerTriangular" | custom-call | tf_op jit(solution)/shard_map/jit(_solve_triangular)/triangular_solve | solution.py:80
  1316.8 39.3 %custom-call.35 = f32[4,128,128]{1,2,0:T(8,128)S(1)} custom-call(f32[4,128,128]{2,1,0:T(8,128)S(1)} %get-tuple-element.34), custom_call_target="InvertDiagBlocksLowerTriangular" | custom-call | tf_op jit(solution)/shard_map/jit(_solve_triangular)/triangular_solve | solution.py:84
  1359.3 78.0 %all-gather.22.cloned.1.call-done = bf16[16384,512]{0,1:T(8,128)(2,1)} async-done(((bf16[4096,512]{0,1:T(8,128)(2,1)}), bf16[16384,512]{0,1:T(8,128)(2,1)}) %all-gather.22.cloned.1.call-update) | async-done | bytes 16777232 | tf_op jit(solution)/shard_map/all_gather | solution.py:33
  1437.4 22.4 %copy.40 = bf16[16384,512]{1,0:T(8,128)(2,1)} copy(bf16[16384,512]{0,1:T(8,128)(2,1)} %all-gather.22.cloned.1.call-done) | data formatting | bytes 33554432 | tf_op jit(solution)/shard_map/all_gather | solution.py:33
  1475.0 135.2 %reduce-scatter.9.cloned.1.call-done = f32[16,512]{1,0:T(8,128)} async-done(((f32[512,512]{1,0:T(8,128)}), f32[16,512]{1,0:T(8,128)}) %reduce-scatter.9.cloned.1.call-update) | async-done | bytes 32784 | tf_op jit(solution)/shard_map/reduce_scatter | solution.py:28
  1611.1 151.1 %all-gather.18.cloned.1.call-done = f32[512,512]{1,0:T(8,128)} async-done(((f32[16,512]{1,0:T(8,128)}), f32[512,512]{1,0:T(8,128)}) %all-gather.18.cloned.1.call-update) | async-done | bytes 1048592 | tf_op jit(solution)/shard_map/all_gather | solution.py:29
  1764.5 11.7 cholesky.358
  1776.9 9.8 custom-call.36
  1787.5 11.7 cholesky.377
  1799.9 10.2 custom-call.37
  1810.8 11.7 cholesky.398
  1823.2 9.8 custom-call.38
  1833.6 11.9 cholesky.415
  1858.5 39.3 %custom-call.39 = f32[4,128,128]{1,2,0:T(8,128)S(1)} custom-call(f32[4,128,128]{2,1,0:T(8,128)S(1)} %get-tuple-element.35), custom_call_target="InvertDiagBlocksLowerTriangular" | custom-call | tf_op jit(solution)/shard_map/jit(_solve_triangular)/triangular_solve | solution.py:80
  1934.6 39.3 %custom-call.40 = f32[4,128,128]{1,2,0:T(8,128)S(1)} custom-call(f32[4,128,128]{2,1,0:T(8,128)S(1)} %get-tuple-element.36), custom_call_target="InvertDiagBlocksLowerTriangular" | custom-call | tf_op jit(solution)/shard_map/jit(_solve_triangular)/triangular_solve | solution.py:84
  1977.1 78.3 %all-gather.26.cloned.1.call-done = bf16[16384,512]{0,1:T(8,128)(2,1)} async-done(((bf16[4096,512]{0,1:T(8,128)(2,1)}), bf16[16384,512]{0,1:T(8,128)(2,1)}) %all-gather.26.cloned.1.call-update) | async-done | bytes 16777232 | tf_op jit(solution)/shard_map/all_gather | solution.py:33
  2055.5 22.6 %copy.41 = bf16[16384,512]{1,0:T(8,128)(2,1)} copy(bf16[16384,512]{0,1:T(8,128)(2,1)} %all-gather.26.cloned.1.call-done) | data formatting | bytes 33554432 | tf_op jit(solution)/shard_map/all_gather | solution.py:33
  2086.9 9.0 subtract_select_fusion
  2095.9 9.1 copy.36
  (190 shorter events, 193.6 us)
Async XLA Ops:
  7.2 37.7 %copy-start = (bf16[1024,1024]{1,0:T(8,128)(2,1)S(1)}, bf16[1024,1024]{1,0:T(8,128)(2,1)}, u32[]{:S(2)}) copy-start(bf16[1024,1024]{1,0:T(8,128)(2,1)} %param.11) | copy-start | bytes 6291460
  7.2 104.7 %all-gather.14.cloned.1.call-start = ((), (), s32[]{:S(2)}) async-start(), calls=%async_computation.3 | async-start | bytes 10485760 | tf_op jit(solution)/shard_map/all_gather | solution.py:51
  48.5 66.2 %copy-start.8 = (s32[4]{0:T(128)S(1)}, s32[4]{0:T(128)}, u32[]{:S(2)}) copy-start(s32[4]{0:T(128)} %param.14) | copy-start | bytes 52
  48.5 773.9 %all-gather.20.cloned.1.call-start = ((), (), s32[]{:S(2)}) async-start(), calls=%async_computation.6 | async-start | bytes 34603008 | tf_op jit(solution)/shard_map/all_gather | solution.py:13
  114.7 879.1 %reduce-scatter.7.cloned.1.call-start = ((), (), s32[]{:S(2)}) async-start(), calls=%async_computation.11 | async-start | bytes 1081344 | tf_op jit(solution)/shard_map/reduce_scatter | solution.py:28
  833.9 10.7 copy-start.7
  841.2 3.4 copy-start.3
  853.7 291.7 %all-gather.16.cloned.1.call-start = ((), (), s32[]{:S(2)}) async-start(), calls=%async_computation.4 | async-start | bytes 1081344 | tf_op jit(solution)/shard_map/all_gather | solution.py:29
  993.8 313.8 %all-gather.24.cloned.1.call-start = ((), (), s32[]{:S(2)}) async-start(), calls=%async_computation.8 | async-start | bytes 5242880 | tf_op jit(solution)/shard_map/all_gather | solution.py:33
  1232.5 204.8 %all-gather.22.cloned.1.call-start = ((), (), s32[]{:S(2)}) async-start(), calls=%async_computation.7 | async-start | bytes 20971520 | tf_op jit(solution)/shard_map/all_gather | solution.py:33
  1304.8 51.4 %copy-start.5 = (f32[512,512]{1,0:T(8,128)S(1)}, f32[512,512]{1,0:T(8,128)}, u32[]{:S(2)}) copy-start(f32[512,512]{1,0:T(8,128)} %all-gather.16.cloned.1.call-done) | copy-start | bytes 3145732
  1304.8 305.4 %reduce-scatter.9.cloned.1.call-start = ((), (), s32[]{:S(2)}) async-start(), calls=%async_computation.12 | async-start | bytes 1081344 | tf_op jit(solution)/shard_map/reduce_scatter | solution.py:28
  1462.2 7.6 copy-start.4
  1469.9 3.4 copy-start.2
  1475.0 287.2 %all-gather.18.cloned.1.call-start = ((), (), s32[]{:S(2)}) async-start(), calls=%async_computation.5 | async-start | bytes 1081344 | tf_op jit(solution)/shard_map/all_gather | solution.py:29
  1610.2 314.7 %all-gather.28.cloned.1.call-start = ((), (), s32[]{:S(2)}) async-start(), calls=%async_computation.10 | async-start | bytes 5242880 | tf_op jit(solution)/shard_map/all_gather | solution.py:33
  1850.2 205.3 %all-gather.26.cloned.1.call-start = ((), (), s32[]{:S(2)}) async-start(), calls=%async_computation.9 | async-start | bytes 20971520 | tf_op jit(solution)/shard_map/all_gather | solution.py:33
  1922.9 51.0 %copy-start.6 = (f32[512,512]{1,0:T(8,128)S(1)}, f32[512,512]{1,0:T(8,128)}, u32[]{:S(2)}) copy-start(f32[512,512]{1,0:T(8,128)} %all-gather.18.cloned.1.call-done) | copy-start | bytes 3145732
  2095.9 9.1 copy-start.1
Sparse Core Ops, SparseCore 0:
  48.7 63.1 all-gather.13
  114.8 707.6 all-gather.19
  853.8 139.9 reduce-scatter.6
  995.4 150.0 all-gather.15
  1232.7 61.1 all-gather.23
  1304.9 132.3 all-gather.21
  1475.1 135.0 reduce-scatter.8
  1611.8 150.3 all-gather.17
  1850.3 61.0 all-gather.27
  1923.1 132.3 all-gather.25
